TPU v7x, 512 devices: a whole 4x4x16 slice. The times are simulated.
512 devices in a mesh: gauss: 128 (over z, x, core), view: 4 (over y).
Axes of the slice: x: 4, y: 4, z: 16, core: 2. Of those that a mesh axis runs over, the one named last changes fastest.
Arguments:
- params: bfloat16 [64, 131072], P(None, 'gauss'), may hold values from -5 to 2, as said below
- lists: int32 [2048, 128], P(('gauss', 'view')), may hold values from -1 to 131071, as said below
- tile_pos: int32 [2048], P(('gauss', 'view')), may hold values from 0 to 255
- cam_index: int32 [2048], P(('gauss', 'view')), may hold values from 0 to 15
- cams: float32 [28, 16], replicated, may hold values from -1 to 1100, as said below
- targets: float32 [3, 2048, 256], P(None, ('gauss', 'view')), may hold values from 0 to 1
Outputs:
- rendered: float32 [3, 2048, 256], P(None, ('gauss', 'view'))
- grads: float32 [64, 131072], P(None, 'gauss')
Inputs may be any that keep to these rules, and one draw needn't show every extreme that they name: `lists`: within each tile the entries that are not -1 come first. The entries of one device's 4 tiles that are not -1 name at most 4 times Gaussians of one gauss index (blocks of 1024 consecutive Gaussians), and in every draw some gauss index is named exactly 4 times by the tiles of every device; the number of entries that are not -1 differs from device to device. `cams`: columns are cameras: rows 0-8 a rotation matrix, 9-11 a translation putting every Gaussian mean at depth 2.4 or more, row 12 the focal length, rows 13-27 appearance weights. `params`: rows 6-9 are quaternions whose first component is 1 or more.
All inputs are finite; a program needn't handle non-finite values.
Results may differ from a plain program's by a relative error of at most 0.0003.
Values may be sent and summed in bfloat16 or wider, within the bound.
A program may use at most 64 MiB of HBM per device.

v0:
```python
import jax
import jax.numpy as jnp
from jax import lax
from jax.sharding import PartitionSpec as P

WIN = 16
HIGH = lax.Precision.HIGHEST


def sh_terms(dir_x, dir_y, dir_z):
    return [
        jnp.ones_like(dir_x),
        dir_x,
        dir_y,
        dir_z,
        dir_x * dir_y,
        dir_y * dir_z,
        dir_x * dir_z,
        dir_x * dir_x - dir_y * dir_y,
        3.0 * dir_z * dir_z - 1.0,
        dir_x * (dir_x * dir_x - 3.0 * dir_y * dir_y),
        dir_x * dir_y * dir_z,
        dir_y * (3.0 * dir_x * dir_x - dir_y * dir_y),
        dir_z * (dir_x * dir_x - dir_y * dir_y),
        dir_x * (5.0 * dir_z * dir_z - 1.0),
        dir_y * (5.0 * dir_z * dir_z - 1.0),
        dir_z * (5.0 * dir_z * dir_z - 3.0),
    ]


def fix_rows(row_vals, is_live):
    return row_vals.at[6].set(jnp.where(is_live, row_vals[6], 1.0))


def project(row_vals, camcols):
    mean_x, mean_y, mean_z = (row_vals[0], row_vals[1], row_vals[2])
    cam_rot = [camcols[index] for index in range(9)]
    focal = camcols[12]
    cam_x = cam_rot[0] * mean_x + cam_rot[1] * mean_y + cam_rot[2] * mean_z + camcols[9]
    cam_y = cam_rot[3] * mean_x + cam_rot[4] * mean_y + cam_rot[5] * mean_z + camcols[10]
    cam_z = cam_rot[6] * mean_x + cam_rot[7] * mean_y + cam_rot[8] * mean_z + camcols[11]
    inv_z = 1.0 / cam_z
    quaternion = row_vals[6:10]
    q_norm = jnp.sqrt(jnp.sum(quaternion * quaternion, axis=0))
    unit_w = quaternion[0] / q_norm
    unit_x = quaternion[1] / q_norm
    unit_y = quaternion[2] / q_norm
    unit_z = quaternion[3] / q_norm
    rotation = [
        [
            1.0 - 2.0 * (unit_y * unit_y + unit_z * unit_z),
            2.0 * (unit_x * unit_y - unit_w * unit_z),
            2.0 * (unit_x * unit_z + unit_w * unit_y),
        ],
        [
            2.0 * (unit_x * unit_y + unit_w * unit_z),
            1.0 - 2.0 * (unit_x * unit_x + unit_z * unit_z),
            2.0 * (unit_y * unit_z - unit_w * unit_x),
        ],
        [
            2.0 * (unit_x * unit_z - unit_w * unit_y),
            2.0 * (unit_y * unit_z + unit_w * unit_x),
            1.0 - 2.0 * (unit_x * unit_x + unit_y * unit_y),
        ],
    ]
    mixed = [
        [
            cam_rot[3 * row_i] * rotation[0][col_k]
            + cam_rot[3 * row_i + 1] * rotation[1][col_k]
            + cam_rot[3 * row_i + 2] * rotation[2][col_k]
            for col_k in range(3)
        ]
        for row_i in range(3)
    ]
    jac_scale = focal * inv_z
    proj_u = [
        jac_scale * mixed[0][col_k] - jac_scale * cam_x * inv_z * mixed[2][col_k]
        for col_k in range(3)
    ]
    proj_v = [
        jac_scale * mixed[1][col_k] - jac_scale * cam_y * inv_z * mixed[2][col_k]
        for col_k in range(3)
    ]
    var_diag = jnp.exp(2.0 * row_vals[3:6])
    cov_a = (
        proj_u[0] * proj_u[0] * var_diag[0]
        + proj_u[1] * proj_u[1] * var_diag[1]
        + proj_u[2] * proj_u[2] * var_diag[2]
        + 0.3
    )
    cov_b = (
        proj_u[0] * proj_v[0] * var_diag[0]
        + proj_u[1] * proj_v[1] * var_diag[1]
        + proj_u[2] * proj_v[2] * var_diag[2]
    )
    cov_c = (
        proj_v[0] * proj_v[0] * var_diag[0]
        + proj_v[1] * proj_v[1] * var_diag[1]
        + proj_v[2] * proj_v[2] * var_diag[2]
        + 0.3
    )
    determinant = cov_a * cov_c - cov_b * cov_b
    opacity = jax.nn.sigmoid(row_vals[10])
    distance = jnp.sqrt(cam_x * cam_x + cam_y * cam_y + cam_z * cam_z)
    terms = sh_terms(cam_x / distance, cam_y / distance, cam_z / distance)
    colors = []
    for chan in range(3):
        shade = 0.5 + sum(
            (row_vals[11 + 16 * chan + basis_b] * terms[basis_b] for basis_b in range(16))
        )
        shade = shade + sum(
            (row_vals[59 + feat_j] * camcols[13 + 3 * feat_j + chan] for feat_j in range(5))
        )
        colors.append(shade)
    centre_u = focal * cam_x * inv_z
    centre_v = focal * cam_y * inv_z
    return jnp.stack(
        [
            centre_u,
            centre_v,
            cov_c / determinant,
            -cov_b / determinant,
            cov_a / determinant,
            opacity,
            colors[0],
            colors[1],
            colors[2],
        ]
    )


def render(attrs, is_live, pixel_x, pixel_y):
    diff_x = pixel_x[None, :] - attrs[0][:, None]
    diff_y = pixel_y[None, :] - attrs[1][:, None]
    power = -0.5 * (
        attrs[2][:, None] * diff_x * diff_x
        + 2.0 * attrs[3][:, None] * diff_x * diff_y
        + attrs[4][:, None] * diff_y * diff_y
    )
    alpha = jnp.where(is_live[:, None], attrs[5][:, None] * jnp.exp(power), 0.0)
    keeping = jnp.cumprod(1.0 - alpha, axis=0)
    transmit = jnp.concatenate([jnp.ones((1, alpha.shape[1]), alpha.dtype), keeping[:-1]], axis=0)
    return jnp.dot(attrs[6:9], alpha * transmit, precision=HIGH)


def pixels(position):
    pixel_idx = jnp.arange(256)
    pixel_x = (16 * (position % WIN - WIN // 2) + pixel_idx % 16).astype(jnp.float32) + 0.5
    pixel_y = (16 * (position // WIN - WIN // 2) + pixel_idx // 16).astype(jnp.float32) + 0.5
    return (pixel_x, pixel_y)


def tile_grads(row_vals, camcol, is_live, pixel_x, pixel_y, target):

    def loss_of(params_in):
        picture = render(project(params_in, camcol[:, None]), is_live, pixel_x, pixel_y)
        return (0.5 * jnp.sum((picture - target) ** 2), picture)

    loss_val, pullback, picture = jax.vjp(loss_of, row_vals, has_aux=True)
    return (picture, pullback(jnp.ones_like(loss_val))[0])


def camera_columns(cams, camera_ids):
    selector = (camera_ids[None, :] == jnp.arange(cams.shape[1])[:, None]).astype(jnp.float32)
    return jnp.dot(cams, selector, precision=HIGH)


def one_tile(rows_in, live_in, camcol, pos_x, pos_y, target):
    return tile_grads(
        fix_rows(rows_in.astype(jnp.float32), live_in), camcol, live_in, pos_x, pos_y, target
    )


def on_device(params, lists, tile_pos, cam_index, cams, targets):
    owners = lax.axis_size("gauss")
    g_dev = params.shape[1]
    width = params.shape[0]
    n_tiles, list_len = lists.shape
    capacity = n_tiles * list_len // owners
    flat_ids = lists.reshape(-1)
    is_live = flat_ids >= 0
    owner_idx = jnp.where(is_live, flat_ids // g_dev, owners)
    selector = (owner_idx[:, None] == jnp.arange(owners)[None, :]).astype(jnp.int32)
    ranks = jnp.sum((jnp.cumsum(selector, axis=0) - selector) * selector, axis=1)
    slot_pos = jnp.where(is_live, owner_idx * capacity + ranks, owners * capacity)
    read_pos = jnp.minimum(slot_pos, owners * capacity - 1)
    local_idx = jnp.where(is_live, flat_ids % g_dev, -1)
    tile_cams = camera_columns(cams, cam_index)
    pixel_x, pixel_y = jax.vmap(pixels)(tile_pos)
    tile_live = is_live.reshape(n_tiles, list_len)
    wanted = (
        jnp.full((owners * capacity,), -1, jnp.int32)
        .at[slot_pos]
        .set(local_idx, mode="drop")
        .reshape(owners, capacity)
    )
    received = lax.all_to_all(wanted, "gauss", split_axis=0, concat_axis=0, tiled=True).reshape(-1)
    received_live = received >= 0
    picked = jnp.take(params, jnp.maximum(received, 0), axis=1)
    returned = lax.all_to_all(
        picked.reshape(width, owners, capacity), "gauss", split_axis=1, concat_axis=1, tiled=True
    )
    slot_rows = jnp.take(returned.reshape(width, -1), read_pos, axis=1).reshape(
        width, n_tiles, list_len
    )
    pictures, tile_g = jax.vmap(one_tile, in_axes=(1, 0, 1, 0, 0, 1), out_axes=(1, 1))(
        slot_rows, tile_live, tile_cams, pixel_x, pixel_y, targets
    )
    slot_g = tile_g.reshape(width, -1)
    sent_g = (
        jnp.zeros((width, owners * capacity), jnp.float32).at[:, slot_pos].set(slot_g, mode="drop")
    )
    row_g = lax.all_to_all(
        sent_g.reshape(width, owners, capacity), "gauss", split_axis=1, concat_axis=1, tiled=True
    ).reshape(width, -1)
    targets_idx = jnp.where(received_live, received, g_dev)
    summed = jnp.zeros((width, g_dev), jnp.float32).at[:, targets_idx].add(row_g, mode="drop")
    grads = lax.psum(summed, "view")
    return (pictures, grads)


def solution(mesh):
    return jax.shard_map(
        on_device,
        mesh=mesh,
        in_specs=(
            P(None, "gauss"),
            P(("gauss", "view"), None),
            P(("gauss", "view")),
            P(("gauss", "view")),
            P(),
            P(None, ("gauss", "view"), None),
        ),
        out_specs=(P(None, ("gauss", "view"), None), P(None, "gauss")),
        check_vma=False,
    )
```

profile of v0, /device:TPU:2, one launch (start us, length us, event | category | flops | bytes accessed | tf_op | source)
XLA Modules:
  0.0 217.4 jit_solution(6644110838534625728)
XLA Ops:
  8.7 2.4 %scatter_custom_fusion = s32[512]{0:T(512)S(1)} fusion(s32[512]{0:T(512)S(1)} %bitcast.784, s32[512]{0:T(512)S(1)} %get-tuple-element.304, s32[]{:T(128)} %constant.170.clone.1), kind=kCustom, calls=%fused_computation.691 | custom fusion | bytes 2052 | tf_op jit(solution)/shard_map/scatter | solution.py:194
  11.9 19.6 %all-to-all-start = ((s32[128,1,4]{2,1,0:T(1,128)}), s32[128,1,4]{2,1,0:T(1,128)S(1)}, u32[]{:S(2)}, u32[]{:S(2)}) async-start(s32[128,1,4]{2,1,0:T(1,128)} %bitcast.8), calls=%async_computation | async-start | bytes 131072 | tf_op jit(solution)/shard_map/all_to_all | solution.py:197
  31.7 1.0 slice_reduce_fusion.15
  34.1 11.2 %all-to-all-done = s32[128,1,4]{2,1,0:T(1,128)S(1)} async-done(((s32[128,1,4]{2,1,0:T(1,128)}), s32[128,1,4]{2,1,0:T(1,128)S(1)}, u32[]{:S(2)}, u32[]{:S(2)}) %all-to-all-start) | async-done | bytes 2080 | tf_op jit(solution)/shard_map/all_to_all | solution.py:197
  45.9 0.8 reduce.61
  47.6 1.3 gather_fusion
  49.9 6.6 %all-to-all-start.1 = ((bf16[128,2,128]{2,1,0:T(2,128)(2,1)}), bf16[128,2,128]{2,1,0:T(2,128)(2,1)S(1)}, u32[]{:S(2)}, u32[]{:S(2)}) async-start(bf16[128,2,128]{2,1,0:T(2,128)(2,1)} %reshape.12609), calls=%async_computation.1 | async-start | bytes 131072 | tf_op jit(solution)/shard_map/all_to_all | solution.py:200
  56.9 13.6 %all-to-all-done.1 = bf16[128,2,128]{2,1,0:T(2,128)(2,1)S(1)} async-done(((bf16[128,2,128]{2,1,0:T(2,128)(2,1)}), bf16[128,2,128]{2,1,0:T(2,128)(2,1)S(1)}, u32[]{:S(2)}, u32[]{:S(2)}) %all-to-all-start.1) | async-done | bytes 65568 | tf_op jit(solution)/shard_map/all_to_all | solution.py:200
  70.6 1.3 gather_fusion.1
  74.4 0.8 fusion.235
  92.9 1.1 fusion.23
  94.0 1.8 fusion.22
  96.6 0.8 slice.660
  97.4 0.9 copy-done.12
  99.4 0.8 copy-done.2
  103.6 0.8 split.66
  109.9 0.8 copy-done.22
  110.7 0.8 copy-done.20
  111.7 0.8 copy-done.9
  112.6 0.9 copy-done.7
  113.7 0.8 fusion.301
  114.7 0.8 copy-done.18
  115.6 0.8 copy-done.17
  117.2 1.5 fusion.13
  121.9 0.9 multiply_multiply_fusion.26
  127.1 0.8 divide_multiply_fusion.2
  128.2 1.9 scatter_custom_fusion.1
  130.3 22.8 %all_to_all.19 = f32[128,1,256]{2,1,0:T(1,128)S(1)} all-to-all(f32[128,1,256]{2,1,0:T(1,128)S(1)} %reshape.12611), channel_id=1, replica_groups=mesh['gauss'=128,'view'=4] {'gauss'}, dimensions={0} | all-to-all | bytes 262144 | tf_op jit(solution)/shard_map/all_to_all | solution.py:213
  153.6 1.0 reduce.62
  154.7 3.2 %scatter_custom_fusion.2 = f32[64,1024]{0,1:T(8,128)} fusion(s32[512]{0:T(512)} %bitcast.783, f32[512,64]{1,0:T(8,128)S(1)} %bitcast.772, f32[]{:T(128)} %constant.184.clone.1), kind=kCustom, calls=%fused_computation.47 | custom fusion | flops 32768 | bytes 262656 | tf_op jit(solution)/shard_map/scatter-add | solution.py:217
  159.2 49.4 %all-reduce.139.cloned.1.call-done = f32[64,1024]{0,1:T(8,128)} async-done(((f32[64,1024]{0,1:T(8,128)}), f32[64,1024]{0,1:T(8,128)}) %all-reduce.139.cloned.1.call-update) | async-done | bytes 262160 | tf_op jit(solution)/shard_map/psum | solution.py:218
  208.6 1.9 copy.288
  (604 shorter events, 46.5 us)
Async XLA Ops:
  7.2 24.3 %copy-start = (f32[28,16]{0,1:T(8,128)S(1)}, f32[28,16]{0,1:T(8,128)}, u32[]{:S(2)}) copy-start(f32[28,16]{0,1:T(8,128)} %param.12) | copy-start | bytes 5380
  7.9 67.9 %copy-start.94 = (pred[4,128]{1,0:T(4,128)(4,1)}, pred[4,128]{1,0:T(4,128)(4,1)S(1)}, u32[]{:S(2)}) copy-start(pred[4,128]{1,0:T(4,128)(4,1)S(1)} %get-tuple-element.152) | copy-start | bytes 1540
  11.1 20.3 %copy-start.199 = (s32[4]{0:T(128)S(1)}, s32[4]{0:T(128)}, u32[]{:S(2)}) copy-start(s32[4]{0:T(128)} %param.11) | copy-start | bytes 52
  11.9 22.1 %copy-start.48 = (bf16[64,1024]{1,0:T(8,128)(2,1)S(1)}, bf16[64,1024]{1,0:T(8,128)(2,1)}, u32[]{:S(2)}) copy-start(bf16[64,1024]{1,0:T(8,128)(2,1)} %param.8) | copy-start | bytes 393220
  11.9 33.5 %all-to-all-start = ((s32[128,1,4]{2,1,0:T(1,128)}), s32[128,1,4]{2,1,0:T(1,128)S(1)}, u32[]{:S(2)}, u32[]{:S(2)}) async-start(s32[128,1,4]{2,1,0:T(1,128)} %bitcast.8), calls=%async_computation | async-start | bytes 131072 | tf_op jit(solution)/shard_map/all_to_all | solution.py:197
  32.7 41.5 %copy-start.56 = (f32[4]{0:T(128)}, f32[4]{0:T(128)S(1)}, u32[]{:S(2)}) copy-start(f32[4]{0:T(128)S(1)} %get-tuple-element.47) | copy-start | bytes 52
  32.7 41.5 %copy-start.63 = (f32[4]{0:T(128)}, f32[4]{0:T(128)S(1)}, u32[]{:S(2)}) copy-start(f32[4]{0:T(128)S(1)} %get-tuple-element.48) | copy-start | bytes 52
  32.7 41.5 %copy-start.138 = (f32[4]{0:T(128)}, f32[4]{0:T(128)S(1)}, u32[]{:S(2)}) copy-start(f32[4]{0:T(128)S(1)} %get-tuple-element.46) | copy-start | bytes 52
  32.7 42.5 %copy-start.85 = (f32[4]{0:T(128)}, f32[4]{0:T(128)S(1)}, u32[]{:S(2)}) copy-start(f32[4]{0:T(128)S(1)} %get-tuple-element.31) | copy-start | bytes 52
  33.0 41.2 %copy-start.58 = (f32[4]{0:T(128)}, f32[4]{0:T(128)S(1)}, u32[]{:S(2)}) copy-start(f32[4]{0:T(128)S(1)} %get-tuple-element.55) | copy-start | bytes 52
  33.0 41.2 %copy-start.61 = (f32[4]{0:T(128)}, f32[4]{0:T(128)S(1)}, u32[]{:S(2)}) copy-start(f32[4]{0:T(128)S(1)} %get-tuple-element.51) | copy-start | bytes 52
  33.0 41.2 %copy-start.65 = (f32[4]{0:T(128)}, f32[4]{0:T(128)S(1)}, u32[]{:S(2)}) copy-start(f32[4]{0:T(128)S(1)} %get-tuple-element.56) | copy-start | bytes 52
  33.0 41.2 %copy-start.68 = (f32[4]{0:T(128)}, f32[4]{0:T(128)S(1)}, u32[]{:S(2)}) copy-start(f32[4]{0:T(128)S(1)} %get-tuple-element.57) | copy-start | bytes 52
  33.1 41.2 %copy-start.71 = (f32[4]{0:T(128)}, f32[4]{0:T(128)S(1)}, u32[]{:S(2)}) copy-start(f32[4]{0:T(128)S(1)} %get-tuple-element.50) | copy-start | bytes 52
  33.1 41.2 %copy-start.73 = (f32[4]{0:T(128)}, f32[4]{0:T(128)S(1)}, u32[]{:S(2)}) copy-start(f32[4]{0:T(128)S(1)} %get-tuple-element.53) | copy-start | bytes 52
  33.1 41.2 %copy-start.83 = (f32[4]{0:T(128)}, f32[4]{0:T(128)S(1)}, u32[]{:S(2)}) copy-start(f32[4]{0:T(128)S(1)} %get-tuple-element.52) | copy-start | bytes 52
  33.1 41.2 %copy-start.140 = (f32[4]{0:T(128)}, f32[4]{0:T(128)S(1)}, u32[]{:S(2)}) copy-start(f32[4]{0:T(128)S(1)} %get-tuple-element.54) | copy-start | bytes 52
  33.1 41.2 %copy-start.143 = (f32[4]{0:T(128)}, f32[4]{0:T(128)S(1)}, u32[]{:S(2)}) copy-start(f32[4]{0:T(128)S(1)} %get-tuple-element.49) | copy-start | bytes 52
  33.8 40.5 %copy-start.196 = (f32[4]{0:T(128)}, f32[4]{0:T(128)S(1)}, u32[]{:S(2)}) copy-start(f32[4]{0:T(128)S(1)} %broadcast_multiply_fusion.24) | copy-start | bytes 52
  33.8 40.4 %copy-start.185 = (f32[4]{0:T(128)}, f32[4]{0:T(128)S(1)}, u32[]{:S(2)}) copy-start(f32[4]{0:T(128)S(1)} %get-tuple-element.308) | copy-start | bytes 52
  33.8 40.4 %copy-start.187 = (f32[4]{0:T(128)}, f32[4]{0:T(128)S(1)}, u32[]{:S(2)}) copy-start(f32[4]{0:T(128)S(1)} %get-tuple-element.309) | copy-start | bytes 52
  33.9 40.4 %copy-start.189 = (f32[4]{0:T(128)}, f32[4]{0:T(128)S(1)}, u32[]{:S(2)}) copy-start(f32[4]{0:T(128)S(1)} %get-tuple-element.310) | copy-start | bytes 52
  33.9 40.4 %copy-start.191 = (f32[4]{0:T(128)}, f32[4]{0:T(128)S(1)}, u32[]{:S(2)}) copy-start(f32[4]{0:T(128)S(1)} %get-tuple-element.311) | copy-start | bytes 52
  33.9 40.4 %copy-start.192 = (f32[4]{0:T(128)}, f32[4]{0:T(128)S(1)}, u32[]{:S(2)}) copy-start(f32[4]{0:T(128)S(1)} %get-tuple-element.312) | copy-start | bytes 52
  33.9 40.4 %copy-start.193 = (f32[4]{0:T(128)}, f32[4]{0:T(128)S(1)}, u32[]{:S(2)}) copy-start(f32[4]{0:T(128)S(1)} %get-tuple-element.313) | copy-start | bytes 52
  33.9 40.4 %copy-start.194 = (f32[4]{0:T(128)}, f32[4]{0:T(128)S(1)}, u32[]{:S(2)}) copy-start(f32[4]{0:T(128)S(1)} %get-tuple-element.314) | copy-start | bytes 52
  33.9 40.4 %copy-start.195 = (f32[4]{0:T(128)}, f32[4]{0:T(128)S(1)}, u32[]{:S(2)}) copy-start(f32[4]{0:T(128)S(1)} %get-tuple-element.315) | copy-start | bytes 52
  49.9 20.6 %all-to-all-start.1 = ((bf16[128,2,128]{2,1,0:T(2,128)(2,1)}), bf16[128,2,128]{2,1,0:T(2,128)(2,1)S(1)}, u32[]{:S(2)}, u32[]{:S(2)}) async-start(bf16[128,2,128]{2,1,0:T(2,128)(2,1)} %reshape.12609), calls=%async_computation.1 | async-start | bytes 131072 | tf_op jit(solution)/shard_map/all_to_all | solution.py:200
  56.6 152.0 %all-reduce.139.cloned.1.call-start = ((), (), s32[]{:S(2)}) async-start(), calls=%async_computation.3 | async-start | bytes 1048576 | tf_op jit(solution)/shard_map/psum | solution.py:218
  56.9 19.0 %copy-start.88 = (f32[4,256]{1,0:T(4,128)}, f32[4,256]{1,0:T(4,128)S(1)}, u32[]{:S(2)}) copy-start(f32[4,256]{1,0:T(4,128)S(1)} %get-tuple-element.316) | copy-start | bytes 12292
  56.9 19.0 %copy-start.91 = (f32[4,256]{1,0:T(4,128)}, f32[4,256]{1,0:T(4,128)S(1)}, u32[]{:S(2)}) copy-start(f32[4,256]{1,0:T(4,128)S(1)} %get-tuple-element.317) | copy-start | bytes 12292
  120.4 4.3 %copy-start.168 = (f32[4]{0:T(128)S(1)}, f32[4]{0:T(128)}, u32[]{:S(2)}) copy-start(f32[4]{0:T(128)} %get-tuple-element.37) | copy-start | bytes 52
  (175 other events, 196.6 us)
Sparse Core Ops, SparseCore 0:
  158.0 50.5 all-reduce.138
where the time goes:
time: 219 us; the launch traced here: 217 us
  waiting for transfers between devices  74.3 us (34%)
  local copies, waits for them, and re-layouts  54.9 us (25%)
  starting transfers between devices  26.4 us (12%)
  blocking collectives  22.8 us (10%)
  other arithmetic  18.4 us (8%)
  between operations  16.9 us (8%)
  matrix products  3.73 us (2%)
    psum x1, waiting for transfers between devices, on_device(): grads = lax.psum(summed, 'view')  49.4 us
    unnamed x411, local copies, waits for them, and re-layouts  38.7 us
    all_to_all x1, blocking collectives, on_device(): lax.all_to_all(sent_g.reshape(width, owners, capacity), 'gauss', split_ax...  22.8 us
    all_to_all x1, starting transfers between devices, on_device(): lax.all_to_all(wanted, 'gauss', split_axis=0, concat_axis=0, tiled=True)  19.6 us
    all_to_all x1, waiting for transfers between devices, on_device(): lax.all_to_all(picked.reshape(width, owners, capacity), 'gauss', split_ax...  13.6 us
    all_to_all x1, waiting for transfers between devices, on_device(): lax.all_to_all(wanted, 'gauss', split_axis=0, concat_axis=0, tiled=True)  11.2 us
    all_to_all x1, starting transfers between devices, on_device(): lax.all_to_all(picked.reshape(width, owners, capacity), 'gauss', split_ax...  6.64 us
  transfers between devices with their start and end apart: 3, of which 3 were waited for; matrix products, arithmetic and copies ran while one was open for 1% of the time, Pallas kernels for 0%

commit v1 on v0

--- a/solution.py
+++ b/solution.py
@@ -2,6 +2,7 @@
 import jax.numpy as jnp
 from jax import lax
 from jax.sharding import PartitionSpec as P
+from jax.lax import all_gather
 
 WIN = 16
 HIGH = lax.Precision.HIGHEST
@@ -215,7 +216,8 @@
     ).reshape(width, -1)
     targets_idx = jnp.where(received_live, received, g_dev)
     summed = jnp.zeros((width, g_dev), jnp.float32).at[:, targets_idx].add(row_g, mode="drop")
-    grads = lax.psum(summed, "view")
+    even = all_gather(summed, "view")
+    grads = jnp.sum(even, axis=0)
     return (pictures, grads)
 
 

time: 219 us -> 193 us (0.88)
  waiting for transfers between devices: 74.3 us -> 47.6 us
    psum x1 -> x0, waiting for transfers between devices: 49.4 us -> none  [on_device(): grads = lax.psum(summed, 'view')]
    all_gather x0 -> x1, waiting for transfers between devices: none -> 22.7 us  [on_device(): even = all_gather(summed, 'view')]
    unnamed x411 -> x410, local copies, waits for them, and re-layouts: 38.7 us -> 36.8 us
where the time goes in v1:
time: 193 us; the launch traced here: 191 us
  local copies, waits for them, and re-layouts  53.9 us (28%)
  waiting for transfers between devices  47.6 us (25%)
  starting transfers between devices  26.4 us (14%)
  blocking collectives  22.8 us (12%)
  other arithmetic  19.7 us (10%)
  between operations  16.9 us (9%)
  matrix products  3.73 us (2%)
    unnamed x410, local copies, waits for them, and re-layouts  36.8 us
    all_to_all x1, blocking collectives, on_device(): lax.all_to_all(sent_g.reshape(width, owners, capacity), 'gauss', split_ax...  22.8 us
    all_gather x1, waiting for transfers between devices, on_device(): even = all_gather(summed, 'view')  22.7 us
    all_to_all x1, starting transfers between devices, on_device(): lax.all_to_all(wanted, 'gauss', split_axis=0, concat_axis=0, tiled=True)  19.6 us
    all_to_all x1, waiting for transfers between devices, on_device(): lax.all_to_all(picked.reshape(width, owners, capacity), 'gauss', split_ax...  13.6 us
    all_to_all x1, waiting for transfers between devices, on_device(): lax.all_to_all(wanted, 'gauss', split_axis=0, concat_axis=0, tiled=True)  11.2 us
    all_to_all x1, starting transfers between devices, on_device(): lax.all_to_all(picked.reshape(width, owners, capacity), 'gauss', split_ax...  6.64 us
  transfers between devices with their start and end apart: 3, of which 3 were waited for; matrix products, arithmetic and copies ran while one was open for 1% of the time, Pallas kernels for 0%

profile of v1, /device:TPU:2, one launch (start us, length us, event | category | flops | bytes accessed | tf_op | source)
XLA Modules:
  0.0 191.0 jit_solution(193808470100192962)
XLA Ops:
  8.7 2.4 %scatter_custom_fusion = s32[512]{0:T(512)S(1)} fusion(s32[512]{0:T(512)S(1)} %bitcast.786, s32[512]{0:T(512)S(1)} %get-tuple-element.304, s32[]{:T(128)} %constant.170.clone.1), kind=kCustom, calls=%fused_computation.691 | custom fusion | bytes 2052 | tf_op jit(solution)/shard_map/scatter | solution.py:195
  11.9 19.6 %all-to-all-start = ((s32[128,1,4]{2,1,0:T(1,128)}), s32[128,1,4]{2,1,0:T(1,128)S(1)}, u32[]{:S(2)}, u32[]{:S(2)}) async-start(s32[128,1,4]{2,1,0:T(1,128)} %bitcast.8), calls=%async_computation | async-start | bytes 131072 | tf_op jit(solution)/shard_map/all_to_all | solution.py:198
  31.7 1.0 slice_reduce_fusion.15
  34.1 11.2 %all-to-all-done = s32[128,1,4]{2,1,0:T(1,128)S(1)} async-done(((s32[128,1,4]{2,1,0:T(1,128)}), s32[128,1,4]{2,1,0:T(1,128)S(1)}, u32[]{:S(2)}, u32[]{:S(2)}) %all-to-all-start) | async-done | bytes 2080 | tf_op jit(solution)/shard_map/all_to_all | solution.py:198
  45.9 0.8 reduce.61
  47.6 1.3 gather_fusion
  49.9 6.6 %all-to-all-start.1 = ((bf16[128,2,128]{2,1,0:T(2,128)(2,1)}), bf16[128,2,128]{2,1,0:T(2,128)(2,1)S(1)}, u32[]{:S(2)}, u32[]{:S(2)}) async-start(bf16[128,2,128]{2,1,0:T(2,128)(2,1)} %reshape.12610), calls=%async_computation.1 | async-start | bytes 131072 | tf_op jit(solution)/shard_map/all_to_all | solution.py:201
  56.9 13.6 %all-to-all-done.1 = bf16[128,2,128]{2,1,0:T(2,128)(2,1)S(1)} async-done(((bf16[128,2,128]{2,1,0:T(2,128)(2,1)}), bf16[128,2,128]{2,1,0:T(2,128)(2,1)S(1)}, u32[]{:S(2)}, u32[]{:S(2)}) %all-to-all-start.1) | async-done | bytes 65568 | tf_op jit(solution)/shard_map/all_to_all | solution.py:201
  70.6 1.3 gather_fusion.1
  74.4 0.8 fusion.235
  92.9 1.1 fusion.23
  94.0 1.8 fusion.22
  96.6 0.8 slice.660
  97.4 0.9 copy-done.12
  99.4 0.8 copy-done.2
  103.6 0.8 split.66
  109.9 0.8 copy-done.22
  110.7 0.8 copy-done.20
  111.7 0.8 copy-done.9
  112.6 0.9 copy-done.7
  113.7 0.8 fusion.301
  114.7 0.8 copy-done.18
  115.6 0.8 copy-done.17
  117.2 1.5 fusion.13
  121.9 0.9 multiply_multiply_fusion.26
  128.2 1.9 scatter_custom_fusion.1
  130.3 22.8 %all_to_all.19 = f32[128,1,256]{2,1,0:T(1,128)S(1)} all-to-all(f32[128,1,256]{2,1,0:T(1,128)S(1)} %reshape.12612), channel_id=1, replica_groups=mesh['gauss'=128,'view'=4] {'gauss'}, dimensions={0} | all-to-all | bytes 262144 | tf_op jit(solution)/shard_map/all_to_all | solution.py:214
  153.6 1.0 reduce.62
  154.7 2.5 %scatter_custom_fusion.2 = f32[64,1024]{0,1:T(8,128)S(1)} fusion(s32[512]{0:T(512)} %bitcast.785, f32[512,64]{1,0:T(8,128)S(1)} %bitcast.774, f32[]{:T(128)} %constant.184.clone.1), kind=kCustom, calls=%fused_computation.47 | custom fusion | flops 32768 | bytes 262656 | tf_op jit(solution)/shard_map/scatter-add | solution.py:218
  157.2 0.9 copy.286
  159.4 22.7 %all-gather.3.cloned.1.call-done = f32[256,1024]{1,0:T(8,128)} async-done(((f32[64,1024]{1,0:T(8,128)}), f32[256,1024]{1,0:T(8,128)}) %all-gather.3.cloned.1.call-update) | async-done | bytes 1048592 | tf_op jit(solution)/shard_map/all_gather | solution.py:219
  182.1 2.0 %reduce_sum.104 = f32[64,1024]{1,0:T(8,128)} reduce(f32[4,64,1024]{2,1,0:T(8,128)} %bitcast.769, f32[]{:T(128)} %constant.184.clone.1), dimensions={0}, to_apply=%region_13.14 | reduce | flops 196608 | bytes 1310724 | tf_op jit(solution)/shard_map/reduce_sum | solution.py:220
  (605 shorter events, 47.3 us)
Async XLA Ops:
  7.2 24.3 %copy-start = (f32[28,16]{0,1:T(8,128)S(1)}, f32[28,16]{0,1:T(8,128)}, u32[]{:S(2)}) copy-start(f32[28,16]{0,1:T(8,128)} %param.12) | copy-start | bytes 5380
  7.9 67.9 %copy-start.94 = (pred[4,128]{1,0:T(4,128)(4,1)}, pred[4,128]{1,0:T(4,128)(4,1)S(1)}, u32[]{:S(2)}) copy-start(pred[4,128]{1,0:T(4,128)(4,1)S(1)} %get-tuple-element.152) | copy-start | bytes 1540
  11.1 20.3 %copy-start.199 = (s32[4]{0:T(128)S(1)}, s32[4]{0:T(128)}, u32[]{:S(2)}) copy-start(s32[4]{0:T(128)} %param.11) | copy-start | bytes 52
  11.9 22.1 %copy-start.48 = (bf16[64,1024]{1,0:T(8,128)(2,1)S(1)}, bf16[64,1024]{1,0:T(8,128)(2,1)}, u32[]{:S(2)}) copy-start(bf16[64,1024]{1,0:T(8,128)(2,1)} %param.8) | copy-start | bytes 393220
  11.9 33.5 %all-to-all-start = ((s32[128,1,4]{2,1,0:T(1,128)}), s32[128,1,4]{2,1,0:T(1,128)S(1)}, u32[]{:S(2)}, u32[]{:S(2)}) async-start(s32[128,1,4]{2,1,0:T(1,128)} %bitcast.8), calls=%async_computation | async-start | bytes 131072 | tf_op jit(solution)/shard_map/all_to_all | solution.py:198
  32.7 41.5 %copy-start.56 = (f32[4]{0:T(128)}, f32[4]{0:T(128)S(1)}, u32[]{:S(2)}) copy-start(f32[4]{0:T(128)S(1)} %get-tuple-element.47) | copy-start | bytes 52
  32.7 41.5 %copy-start.63 = (f32[4]{0:T(128)}, f32[4]{0:T(128)S(1)}, u32[]{:S(2)}) copy-start(f32[4]{0:T(128)S(1)} %get-tuple-element.48) | copy-start | bytes 52
  32.7 41.5 %copy-start.138 = (f32[4]{0:T(128)}, f32[4]{0:T(128)S(1)}, u32[]{:S(2)}) copy-start(f32[4]{0:T(128)S(1)} %get-tuple-element.46) | copy-start | bytes 52
  32.7 42.5 %copy-start.85 = (f32[4]{0:T(128)}, f32[4]{0:T(128)S(1)}, u32[]{:S(2)}) copy-start(f32[4]{0:T(128)S(1)} %get-tuple-element.31) | copy-start | bytes 52
  33.0 41.2 %copy-start.58 = (f32[4]{0:T(128)}, f32[4]{0:T(128)S(1)}, u32[]{:S(2)}) copy-start(f32[4]{0:T(128)S(1)} %get-tuple-element.55) | copy-start | bytes 52
  33.0 41.2 %copy-start.61 = (f32[4]{0:T(128)}, f32[4]{0:T(128)S(1)}, u32[]{:S(2)}) copy-start(f32[4]{0:T(128)S(1)} %get-tuple-element.51) | copy-start | bytes 52
  33.0 41.2 %copy-start.65 = (f32[4]{0:T(128)}, f32[4]{0:T(128)S(1)}, u32[]{:S(2)}) copy-start(f32[4]{0:T(128)S(1)} %get-tuple-element.56) | copy-start | bytes 52
  33.0 41.2 %copy-start.68 = (f32[4]{0:T(128)}, f32[4]{0:T(128)S(1)}, u32[]{:S(2)}) copy-start(f32[4]{0:T(128)S(1)} %get-tuple-element.57) | copy-start | bytes 52
  33.1 41.2 %copy-start.71 = (f32[4]{0:T(128)}, f32[4]{0:T(128)S(1)}, u32[]{:S(2)}) copy-start(f32[4]{0:T(128)S(1)} %get-tuple-element.50) | copy-start | bytes 52
  33.1 41.2 %copy-start.73 = (f32[4]{0:T(128)}, f32[4]{0:T(128)S(1)}, u32[]{:S(2)}) copy-start(f32[4]{0:T(128)S(1)} %get-tuple-element.53) | copy-start | bytes 52
  33.1 41.2 %copy-start.83 = (f32[4]{0:T(128)}, f32[4]{0:T(128)S(1)}, u32[]{:S(2)}) copy-start(f32[4]{0:T(128)S(1)} %get-tuple-element.52) | copy-start | bytes 52
  33.1 41.2 %copy-start.140 = (f32[4]{0:T(128)}, f32[4]{0:T(128)S(1)}, u32[]{:S(2)}) copy-start(f32[4]{0:T(128)S(1)} %get-tuple-element.54) | copy-start | bytes 52
  33.1 41.2 %copy-start.143 = (f32[4]{0:T(128)}, f32[4]{0:T(128)S(1)}, u32[]{:S(2)}) copy-start(f32[4]{0:T(128)S(1)} %get-tuple-element.49) | copy-start | bytes 52
  33.8 40.5 %copy-start.196 = (f32[4]{0:T(128)}, f32[4]{0:T(128)S(1)}, u32[]{:S(2)}) copy-start(f32[4]{0:T(128)S(1)} %broadcast_multiply_fusion.24) | copy-start | bytes 52
  33.8 40.4 %copy-start.185 = (f32[4]{0:T(128)}, f32[4]{0:T(128)S(1)}, u32[]{:S(2)}) copy-start(f32[4]{0:T(128)S(1)} %get-tuple-element.308) | copy-start | bytes 52
  33.8 40.4 %copy-start.187 = (f32[4]{0:T(128)}, f32[4]{0:T(128)S(1)}, u32[]{:S(2)}) copy-start(f32[4]{0:T(128)S(1)} %get-tuple-element.309) | copy-start | bytes 52
  33.9 40.4 %copy-start.189 = (f32[4]{0:T(128)}, f32[4]{0:T(128)S(1)}, u32[]{:S(2)}) copy-start(f32[4]{0:T(128)S(1)} %get-tuple-element.310) | copy-start | bytes 52
  33.9 40.4 %copy-start.191 = (f32[4]{0:T(128)}, f32[4]{0:T(128)S(1)}, u32[]{:S(2)}) copy-start(f32[4]{0:T(128)S(1)} %get-tuple-element.311) | copy-start | bytes 52
  33.9 40.4 %copy-start.192 = (f32[4]{0:T(128)}, f32[4]{0:T(128)S(1)}, u32[]{:S(2)}) copy-start(f32[4]{0:T(128)S(1)} %get-tuple-element.312) | copy-start | bytes 52
  33.9 40.4 %copy-start.193 = (f32[4]{0:T(128)}, f32[4]{0:T(128)S(1)}, u32[]{:S(2)}) copy-start(f32[4]{0:T(128)S(1)} %get-tuple-element.313) | copy-start | bytes 52
  33.9 40.4 %copy-start.194 = (f32[4]{0:T(128)}, f32[4]{0:T(128)S(1)}, u32[]{:S(2)}) copy-start(f32[4]{0:T(128)S(1)} %get-tuple-element.314) | copy-start | bytes 52
  33.9 40.4 %copy-start.195 = (f32[4]{0:T(128)}, f32[4]{0:T(128)S(1)}, u32[]{:S(2)}) copy-start(f32[4]{0:T(128)S(1)} %get-tuple-element.315) | copy-start | bytes 52
  49.9 20.6 %all-to-all-start.1 = ((bf16[128,2,128]{2,1,0:T(2,128)(2,1)}), bf16[128,2,128]{2,1,0:T(2,128)(2,1)S(1)}, u32[]{:S(2)}, u32[]{:S(2)}) async-start(bf16[128,2,128]{2,1,0:T(2,128)(2,1)} %reshape.12610), calls=%async_computation.1 | async-start | bytes 131072 | tf_op jit(solution)/shard_map/all_to_all | solution.py:201
  56.6 125.6 %all-gather.3.cloned.1.call-start = ((), (), s32[]{:S(2)}) async-start(), calls=%async_computation.3 | async-start | bytes 1310720 | tf_op jit(solution)/shard_map/all_gather | solution.py:219
  56.9 19.0 %copy-start.88 = (f32[4,256]{1,0:T(4,128)}, f32[4,256]{1,0:T(4,128)S(1)}, u32[]{:S(2)}) copy-start(f32[4,256]{1,0:T(4,128)S(1)} %get-tuple-element.316) | copy-start | bytes 12292
  56.9 19.0 %copy-start.91 = (f32[4,256]{1,0:T(4,128)}, f32[4,256]{1,0:T(4,128)S(1)}, u32[]{:S(2)}) copy-start(f32[4,256]{1,0:T(4,128)S(1)} %get-tuple-element.317) | copy-start | bytes 12292
  120.4 4.3 %copy-start.168 = (f32[4]{0:T(128)S(1)}, f32[4]{0:T(128)}, u32[]{:S(2)}) copy-start(f32[4]{0:T(128)} %get-tuple-element.37) | copy-start | bytes 52
  (175 other events, 196.6 us)
Sparse Core Ops, SparseCore 0:
  158.2 23.8 all-gather.2
